TPU v7x, 32 devices: a whole 2x2x4 slice. The times are simulated.
32 devices in a mesh: mem: 4 (over z), tile: 8 (over y, x, core).
Axes of the slice: x: 2, y: 2, z: 4, core: 2. Of those that a mesh axis runs over, the one named last changes fastest.
Arguments:
- state: float32 [20, 8, 12960], P('mem', 'tile'), may hold values from -6 to 6
- obs_index: int32 [8, 256], P('tile'), may hold values from 0 to 12959
- obs_count: int32 [8], P('tile'), may hold values from 32 to 256, as said below
- obs_value: float32 [8, 256], P('tile'), may hold values from -8 to 8
- obs_rinv: float32 [8, 256], P('tile'), may hold values from 0.1 to 1
- radius: int32 [8], P('tile'), may hold values from 1 to 2
Outputs:
- analysis: float32 [20, 8, 12960], P('mem', 'tile')
Inputs may be any that keep to these rules, and one draw needn't show every extreme that they name: `obs_count`: at most 256; some tile has exactly 256 in every draw.
All inputs are finite; a program needn't handle non-finite values.
Results may differ from a plain program's by a relative error of at most 0.0003.
Values sent between devices are 32-bit elements; how exact they have to be, the bound alone decides.
A program may use at most 64 MiB of HBM per device.

v0:
```python
import jax
import jax.numpy as jnp
from jax import lax
from jax.sharding import PartitionSpec as P

COLS = 45
BLOCK = 9
HALO = 2
NS_ITERS = 4


highest = lax.Precision.HIGHEST


def shifted(block, axis, distance):
    devices = range(lax.axis_size(axis))
    route = [((i - distance) % len(devices), i) for i in devices]
    return lax.ppermute(block, axis, route)


def block_points(band_id, tile_id, rows_dev):
    half_block = (BLOCK - 1) // 2
    row_blocks = rows_dev // BLOCK
    col_blocks = COLS // BLOCK
    row_ids = band_id * rows_dev + BLOCK * jnp.arange(row_blocks, dtype=jnp.int32) + half_block
    col_ids = tile_id * COLS + BLOCK * jnp.arange(col_blocks, dtype=jnp.int32) + half_block
    point_rows = (
        jnp.broadcast_to(row_ids[:, None], (row_blocks, col_blocks)).reshape(-1).astype(jnp.float32)
    )
    point_cols = (
        jnp.broadcast_to(col_ids[None, :], (row_blocks, col_blocks)).reshape(-1).astype(jnp.float32)
    )
    return (point_rows, point_cols)


def locality(obs_meta, point_rows, point_cols, extent, circle):
    row_gap = jnp.abs(obs_meta[2][None, :] - point_rows[:, None])
    col_gap = jnp.abs(obs_meta[3][None, :] - point_cols[:, None])
    col_gap = jnp.minimum(col_gap, circle - col_gap)
    taper = jnp.maximum(0.0, 1.0 - row_gap / extent) * jnp.maximum(0.0, 1.0 - col_gap / extent)
    return taper * obs_meta[1][None, :]


def add_block(totals, ens_blk, meta_blk, point_rows, point_cols, extent, circle):
    gram_sum, rhs_sum = totals
    centre = jnp.mean(ens_blk, axis=0)
    spread_obs = ens_blk - centre[None, :]
    innovation = meta_blk[0] - centre
    weights = locality(meta_blk, point_rows, point_cols, extent, circle)
    weighted = weights[:, None, :] * spread_obs[None, :, :]
    gram_sum = gram_sum + jnp.einsum("pkj,lj->pkl", weighted, spread_obs, precision=highest)
    rhs_sum = rhs_sum + jnp.einsum("pkj,j->pk", weighted, innovation, precision=highest)
    return (gram_sum, rhs_sum)


def transform(gram_sum, rhs_sum, members):
    identity = jnp.eye(members, dtype=jnp.float32)
    gram_full = gram_sum + (members - 1.0) * identity[None]
    frob_norm = jnp.sqrt(jnp.sum(gram_full * gram_full, axis=(1, 2)))
    iterate = gram_full / frob_norm[:, None, None]
    inv_root = jnp.broadcast_to(identity, gram_full.shape)
    for sweep in range(NS_ITERS):
        middle = 1.5 * identity[None] - 0.5 * jnp.einsum(
            "pij,pjk->pik", inv_root, iterate, precision=highest
        )
        iterate = jnp.einsum("pij,pjk->pik", iterate, middle, precision=highest)
        inv_root = jnp.einsum("pij,pjk->pik", middle, inv_root, precision=highest)
    inv_root = inv_root / jnp.sqrt(frob_norm)[:, None, None]
    inner = jnp.einsum("pij,pj->pi", inv_root, rhs_sum, precision=highest)
    mean_shift = jnp.einsum("pij,pj->pi", inv_root, inner, precision=highest)
    return jnp.sqrt(members - 1.0) * inv_root + mean_shift[:, :, None]


def apply_mix(band_state, mixing, rows_dev):
    members = band_state.shape[0]
    row_blocks = rows_dev // BLOCK
    col_blocks = COLS // BLOCK
    cell_grid = band_state.reshape(members, row_blocks, BLOCK, col_blocks, BLOCK)
    centre = jnp.mean(cell_grid, axis=0)
    spread_state = cell_grid - centre[None]
    mix_blocks = mixing.reshape(row_blocks, col_blocks, members, members)
    result = (
        jnp.einsum("ablk,laibj->kaibj", mix_blocks, spread_state, precision=highest) + centre[None]
    )
    return result.reshape(members, rows_dev * COLS)


def shards(state, obs_index, obs_count, obs_value, obs_rinv, radius):
    groups = lax.axis_size("mem")
    tile_count = lax.axis_size("tile")
    mem_dev = state.shape[0]
    cell_count = state.shape[2]
    members = mem_dev * groups
    band_cells = cell_count // groups
    rows_dev = band_cells // COLS
    circle = 1.0 * COLS * tile_count
    tile_id = lax.axis_index("tile")
    band_id = lax.axis_index("mem")
    slot_count = obs_index.shape[1]
    own_state = state[:, 0, :]
    cell_index = obs_index[0]
    own_obs = jnp.take(own_state, cell_index, axis=1)
    slot_ids = jnp.arange(slot_count, dtype=jnp.int32)
    rinv_live = jnp.where(slot_ids < obs_count[0], obs_rinv[0], 0.0)
    obs_row = (cell_index // COLS).astype(jnp.float32)
    obs_col = (cell_index % COLS + tile_id * COLS).astype(jnp.float32)
    obs_meta = jnp.stack([obs_value[0], rinv_live, obs_row, obs_col])
    offsets = [distance * direction for distance in range(1, HALO + 1) for direction in (1, -1)]
    ensemble = lax.all_gather(own_obs, "mem", axis=0, tiled=True)
    local_rows = jnp.concatenate([ensemble, obs_meta], axis=0)
    pieces = [local_rows]
    for offset in offsets:
        pieces.append(shifted(local_rows, "tile", offset))
    window = jnp.concatenate(pieces, axis=1)
    ens_win = window[:members]
    meta_win = window[members:]
    spread = state.reshape(mem_dev, groups, band_cells)
    gathered_state = lax.all_to_all(spread, "mem", split_axis=1, concat_axis=0, tiled=True)
    point_rows, point_cols = block_points(band_id, tile_id, rows_dev)
    extent = (radius[0] * COLS).astype(jnp.float32)
    points = point_rows.shape[0]
    stride = min(128, slot_count)
    per_piece = slot_count // stride
    segments = len(pieces)
    totals = (
        jnp.zeros((points, members, members), jnp.float32),
        jnp.zeros((points, members), jnp.float32),
    )

    def visit(block_id, carried):
        first_col = block_id * stride
        ens_blk = lax.dynamic_slice_in_dim(ens_win, first_col, stride, 1)
        meta_blk = lax.dynamic_slice_in_dim(meta_win, first_col, stride, 1)
        return add_block(carried, ens_blk, meta_blk, point_rows, point_cols, extent, circle)

    for segment in range(segments):
        weights_row = meta_win[1, segment * slot_count : (segment + 1) * slot_count]
        filled = jnp.sum((weights_row > 0.0).astype(jnp.int32))
        opening = segment * per_piece
        totals = lax.fori_loop(opening, opening + (filled + stride - 1) // stride, visit, totals)
    mixing = transform(totals[0], totals[1], members)
    analysis = apply_mix(gathered_state[:, 0, :], mixing, rows_dev)
    returned = lax.all_to_all(analysis[:, None, :], "mem", split_axis=0, concat_axis=1, tiled=True)
    return returned.reshape(mem_dev, 1, cell_count)


def solution(mesh):
    in_specs = (
        P("mem", "tile", None),
        P("tile", None),
        P("tile"),
        P("tile", None),
        P("tile", None),
        P("tile"),
    )
    out_specs = P("mem", "tile", None)
    return jax.shard_map(shards, mesh=mesh, in_specs=in_specs, out_specs=out_specs, check_vma=False)
```

profile of v0, /device:TPU:5, one launch (start us, length us, event | category | flops | bytes accessed | tf_op | source)
XLA Modules:
  0.0 104.6 jit_solution(1941645143184801129)
XLA Ops:
  0.7 5.1 %copy.32 = f32[5,1,12960]{0,2,1:T(8,128)} copy(f32[5,1,12960]{2,1,0:T(1,128)} %param.16) | data formatting | bytes 518400 | tf_op args[0]
  5.8 3.6 %gather_fusion = f32[256,5]{1,0:T(8,128)S(1)} fusion(f32[5,12960]{0,1:T(8,128)} %bitcast.212, s32[1024]{0:T(1024)S(1)} %pad_clamp_fusion), kind=kCustom, calls=%fused_computation | custom fusion | bytes 11264 | tf_op jit(solution)/shard_map/jit(_take)/gather | solution.py:102
  9.6 10.8 %all-gather = f32[4,5,256]{2,1,0:T(8,128)S(1)} all-gather(f32[1,5,256]{2,1,0:T(8,128)S(1)} %copy.33), channel_id=1, replica_groups=mesh['mem'=4,'tile'=8] {'mem'}, dimensions={0}, use_global_device_ids=true | all-gather | bytes 25600 | tf_op jit(solution)/shard_map/all_gather | solution.py:109
  20.4 0.7 fusion.110
  21.1 1.2 %collective-permute-start.3 = (f32[24,256]{1,0:T(8,128)S(1)}, f32[24,256]{1,0:T(8,128)S(1)}, u32[]{:S(2)}, u32[]{:S(2)}) collective-permute-start(f32[24,256]{1,0:T(8,128)S(1)} %concatenate.6), channel_id=1, source_target_pairs={{2,0},{3,1},{4,2},{5,3},{6,4},{7,5},{0,6},{1,7},{10,8},{11,9},{12,... | collective-permute-start | bytes 73736 | tf_op jit(solution)/shard_map/ppermute | solution.py:18
  22.7 3.8 %collective-permute-start.1 = (f32[24,256]{1,0:T(8,128)S(1)}, f32[24,256]{1,0:T(8,128)S(1)}, u32[]{:S(2)}, u32[]{:S(2)}) collective-permute-start(f32[24,256]{1,0:T(8,128)S(1)} %concatenate.6), channel_id=1, source_target_pairs={{1,0},{2,1},{3,2},{4,3},{5,4},{6,5},{7,6},{0,7},{9,8},{10,9},{11,1... | collective-permute-start | bytes 73736 | tf_op jit(solution)/shard_map/ppermute | solution.py:18
  26.5 2.0 %collective-permute-start = (f32[24,256]{1,0:T(8,128)S(1)}, f32[24,256]{1,0:T(8,128)S(1)}, u32[]{:S(2)}, u32[]{:S(2)}) collective-permute-start(f32[24,256]{1,0:T(8,128)S(1)} %concatenate.6), channel_id=1, source_target_pairs={{7,0},{0,1},{1,2},{2,3},{3,4},{4,5},{5,6},{6,7},{15,8},{8,9},{9,10... | collective-permute-start | bytes 73736 | tf_op jit(solution)/shard_map/ppermute | solution.py:18
  28.5 0.6 reduce.8
  29.4 0.8 copy.29
  30.2 4.3 %all-to-all-start = ((f32[5,4,3240]{2,0,1:T(8,128)}), f32[5,4,3240]{2,0,1:T(8,128)S(1)}, u32[]{:S(2)}, u32[]{:S(2)}) async-start(f32[5,4,3240]{2,0,1:T(8,128)} %copy.29), calls=%async_computation | async-start | bytes 851968 | tf_op jit(solution)/shard_map/all_to_all | solution.py:118
  36.0 0.7 fusion.116
  36.7 0.6 fusion.115
  37.3 0.7 fusion.114
  40.0 0.7 fusion.113
  41.6 2.6 %while.65 = (s32[]{:T(128)}, f32[40,20,20]{0,2,1:T(8,128)S(1)}, f32[40,20]{0,1:T(8,128)S(1)}, s32[]{:T(128)}, f32[4,1280]{1,0:T(4,128)S(1)}, /*index=5*/f32[]{:T...) while((s32[]{:T(128)}, f32[40,20,20]{0,2,1:T(8,128)S(1)}, ...), condition=%wide.region_4.5_spmd.clone, body=%wide.region_2.4_spmd.clone.sunk | while | flops 26103460 | bytes 275183 | solution.py:140
  42.7 1.5 %convolution_add_fusion.10 = f32[40,20,20]{0,2,1:T(8,128)S(1)} fusion(f32[40,20,20]{0,2,1:T(8,128)S(1)} %get-tuple-element.817, f32[20,128]{1,0:T(8,128)S(1)} %dynamic-slice_subtract_fusion.10, f32[40,128]{1,0:T(8,128)S(1)} %fusion.183), kind=kOutput, calls=%fused_computation.11.clone.1 | convolution fusion | flops 24694400 | bytes 158720 | tf_op jit(solution)/shard_map/while/body/pkj,lj->pkl/dot_general | solution.py:51
  44.2 2.6 %while.66 = (s32[]{:T(128)}, f32[40,20,20]{0,2,1:T(8,128)S(1)}, f32[40,20]{0,1:T(8,128)S(1)}, s32[]{:T(128)}, f32[4,1280]{1,0:T(4,128)S(1)}, /*index=5*/f32[]{:T...) while((s32[]{:T(128)}, f32[40,20,20]{0,2,1:T(8,128)S(1)}, ...), condition=%wide.region_8.9_spmd.clone, body=%wide.region_6.8_spmd.clone.sunk | while | flops 26103460 | bytes 275183 | solution.py:140
  45.3 1.5 %convolution_add_fusion.11 = f32[40,20,20]{0,2,1:T(8,128)S(1)} fusion(f32[40,20,20]{0,2,1:T(8,128)S(1)} %get-tuple-element.856, f32[20,128]{1,0:T(8,128)S(1)} %dynamic-slice_subtract_fusion.11, f32[40,128]{1,0:T(8,128)S(1)} %fusion.189), kind=kOutput, calls=%fused_computation.37.clone.1 | convolution fusion | flops 24694400 | bytes 158720 | tf_op jit(solution)/shard_map/while/body/pkj,lj->pkl/dot_general | solution.py:51
  46.9 2.6 %while.67 = (s32[]{:T(128)}, f32[40,20,20]{0,2,1:T(8,128)S(1)}, f32[40,20]{0,1:T(8,128)S(1)}, s32[]{:T(128)}, f32[4,1280]{1,0:T(4,128)S(1)}, /*index=5*/f32[]{:T...) while((s32[]{:T(128)}, f32[40,20,20]{0,2,1:T(8,128)S(1)}, ...), condition=%wide.region_12.13_spmd.clone, body=%wide.region_10.12_spmd.clone.sunk | while | flops 26103460 | bytes 275183 | solution.py:140
  48.0 1.5 %convolution_add_fusion.12 = f32[40,20,20]{0,2,1:T(8,128)S(1)} fusion(f32[40,20,20]{0,2,1:T(8,128)S(1)} %get-tuple-element.895, f32[20,128]{1,0:T(8,128)S(1)} %dynamic-slice_subtract_fusion.12, f32[40,128]{1,0:T(8,128)S(1)} %fusion.195), kind=kOutput, calls=%fused_computation.63.clone.1 | convolution fusion | flops 24694400 | bytes 158720 | tf_op jit(solution)/shard_map/while/body/pkj,lj->pkl/dot_general | solution.py:51
  49.5 5.3 %while.68 = (s32[]{:T(128)}, f32[40,20,20]{0,2,1:T(8,128)S(1)}, f32[40,20]{0,1:T(8,128)S(1)}, s32[]{:T(128)}, f32[4,1280]{1,0:T(4,128)S(1)}, /*index=5*/f32[]{:T...) while((s32[]{:T(128)}, f32[40,20,20]{0,2,1:T(8,128)S(1)}, ...), condition=%wide.region_16.17_spmd.clone, body=%wide.region_14.16_spmd.clone.sunk | while | flops 26103460 | bytes 275183 | solution.py:140
  50.6 1.5 %convolution_add_fusion.13 = f32[40,20,20]{0,2,1:T(8,128)S(1)} fusion(f32[40,20,20]{0,2,1:T(8,128)S(1)} %get-tuple-element.934, f32[20,128]{1,0:T(8,128)S(1)} %dynamic-slice_subtract_fusion.13, f32[40,128]{1,0:T(8,128)S(1)} %fusion.201), kind=kOutput, calls=%fused_computation.89.clone.1 | convolution fusion | flops 24694400 | bytes 158720 | tf_op jit(solution)/shard_map/while/body/pkj,lj->pkl/dot_general | solution.py:51
  53.3 1.5 %convolution_add_fusion.13 = f32[40,20,20]{0,2,1:T(8,128)S(1)} fusion(f32[40,20,20]{0,2,1:T(8,128)S(1)} %get-tuple-element.934, f32[20,128]{1,0:T(8,128)S(1)} %dynamic-slice_subtract_fusion.13, f32[40,128]{1,0:T(8,128)S(1)} %fusion.201), kind=kOutput, calls=%fused_computation.89.clone.1 | convolution fusion | flops 24694400 | bytes 158720 | tf_op jit(solution)/shard_map/while/body/pkj,lj->pkl/dot_general | solution.py:51
  54.8 2.8 %while.69 = (s32[]{:T(128)}, f32[40,20,20]{0,2,1:T(8,128)S(1)}, f32[40,20]{0,1:T(8,128)S(1)}, s32[]{:T(128)}, f32[4,1280]{1,0:T(4,128)S(1)}, /*index=5*/f32[]{:T...) while((s32[]{:T(128)}, f32[40,20,20]{0,2,1:T(8,128)S(1)}, ...), condition=%wide.region_20.21_spmd.clone, body=%wide.region_18.20_spmd.clone.sunk | while | flops 26103460 | bytes 275183 | solution.py:140
  55.9 1.5 %convolution_add_fusion.14 = f32[40,20,20]{0,2,1:T(8,128)S(1)} fusion(f32[40,20,20]{0,2,1:T(8,128)S(1)} %get-tuple-element.973, f32[20,128]{1,0:T(8,128)S(1)} %dynamic-slice_subtract_fusion.14, f32[40,128]{1,0:T(8,128)S(1)} %fusion.207), kind=kOutput, calls=%fused_computation.115.clone.1 | convolution fusion | flops 24694400 | bytes 158720 | tf_op jit(solution)/shard_map/while/body/pkj,lj->pkl/dot_general | solution.py:51
  58.2 0.9 fusion.103
  59.1 0.9 fusion.118
  60.0 0.9 fusion.104
  60.9 0.9 fusion.102
  61.8 0.9 fusion.120
  62.7 0.9 fusion.119
  63.7 0.9 fusion.101
  64.6 0.9 fusion.122
  65.5 0.9 fusion.121
  66.5 0.9 fusion.100
  67.4 0.9 convolution_divide_fusion
  68.4 0.9 convolution_bitcast_fusion
  69.3 1.1 %fusion.123 = f32[40,1,20]{2,1,0:T(1,128)S(1)} fusion(f32[40,20,20]{2,1,0:T(8,128)S(1)} %convolution_divide_fusion, f32[40,20,1]{1,2,0:T(1,128)S(1)} %convolution_bitcast_fusion), kind=kOutput, calls=%fused_computation.200 | convolution fusion | flops 192000 | bytes 70400 | tf_op jit(solution)/shard_map/pij,pj->pi/dot_general | solution.py:70
  70.3 1.0 multiply_add_fusion
  71.3 0.8 copy-done
  72.0 3.7 %reshape_squeeze.3 = f32[20,8,9,5,9]{4,3,2,1,0:T(8,128)} reshape(f32[4,5,1,3240]{3,1,0,2:T(8,128)S(1)} %bitcast.213) | data formatting | bytes 518400 | tf_op jit(solution)/shard_map/reshape;squeeze | solution.py:78
  75.7 4.9 %copy.31 = f32[20,8,9,5,9]{0,4,2,3,1:T(8,128)S(1)} copy(f32[20,8,9,5,9]{4,3,2,1,0:T(8,128)} %reshape_squeeze.3) | data formatting | bytes 518400 | tf_op jit(solution)/shard_map/reshape;squeeze | solution.py:78
  80.7 1.1 %reduce_sum.108 = f32[3240]{0:T(1024)S(1)} reduce(f32[5,4,3240]{2,0,1:T(8,128)} %copy-done, f32[]{:T(128)} %constant.197.clone.1), dimensions={0,1}, to_apply=%region_0.1 | reduce | flops 61560 | bytes 272164 | tf_op jit(solution)/shard_map/reduce_sum | solution.py:79
  82.0 4.5 %bitcast_add_fusion.5 = f32[20,8,9,5,9]{0,4,2,3,1:T(8,128)S(1)} fusion(f32[8,5,20,20,1]{3,2,4,1,0:T(8,128)} %bitcast.215, f32[20,8,9,5,9]{0,4,2,3,1:T(8,128)S(1)} %copy.31, f32[8,9,5,9]{3,1,2,0:T(8,128)S(1)} %copy.30), kind=kOutput, calls=%fused_computation.141 | convolution fusion | flops 15681600 | bytes 595360 | tf_op jit(solution)/shard_map/ablk,laibj->kaibj/dot_general | solution.py:83
  86.7 1.4 %broadcast_in_dim_reshape.3 = f32[20,1,3240]{0,2,1:T(8,128)} reshape(f32[20,8,9,5,9]{0,4,3,2,1:T(8,128)S(1)} %copy.36) | data formatting | bytes 518400 | tf_op jit(solution)/shard_map/broadcast_in_dim;reshape | solution.py:143
  88.1 1.8 %copy.37 = f32[20,1,3240]{2,1,0:T(1,128)S(1)} copy(f32[20,1,3240]{0,2,1:T(8,128)} %broadcast_in_dim_reshape.3) | data formatting | bytes 518400 | tf_op jit(solution)/shard_map/broadcast_in_dim;reshape | solution.py:143
  89.9 13.5 %all_to_all.30 = f32[20,1,3240]{2,1,0:T(1,128)S(1)} all-to-all(f32[20,1,3240]{2,1,0:T(1,128)S(1)} %copy.37), channel_id=1, replica_groups=mesh['mem'=4,'tile'=8] {'mem'}, dimensions={0} | all-to-all | bytes 518400 | tf_op jit(solution)/shard_map/all_to_all | solution.py:143
  103.5 1.2 %reshape.499 = f32[5,1,12960]{2,1,0:T(1,128)} reshape(f32[5,4,1,3240]{3,1,2,0:T(4,128)S(1)} %copy.38) | data formatting | bytes 518400 | tf_op jit(solution)/shard_map/reshape | solution.py:144
  (124 shorter events, 8.3 us)
Async XLA Ops:
  0.7 5.1 %copy-start.2 = (s32[1,256]{1,0:T(1,128)S(1)}, s32[1,256]{1,0:T(1,128)}, u32[]{:S(2)}) copy-start(s32[1,256]{1,0:T(1,128)} %param.17) | copy-start | bytes 3076
  0.7 19.7 %copy-start.3 = (f32[1,256]{1,0:T(1,128)S(1)}, f32[1,256]{1,0:T(1,128)}, u32[]{:S(2)}) copy-start(f32[1,256]{1,0:T(1,128)} %param.20) | copy-start | bytes 3076
  0.7 20.4 %copy-start.4 = (f32[1,256]{1,0:T(1,128)S(1)}, f32[1,256]{1,0:T(1,128)}, u32[]{:S(2)}) copy-start(f32[1,256]{1,0:T(1,128)} %param.19) | copy-start | bytes 3076
  0.7 27.8 %copy-start.1 = (f32[5,1,12960]{2,1,0:T(1,128)S(1)}, f32[5,1,12960]{2,1,0:T(1,128)}, u32[]{:S(2)}) copy-start(f32[5,1,12960]{2,1,0:T(1,128)} %param.16) | copy-start | bytes 777604
  21.1 14.8 %collective-permute-start.3 = (f32[24,256]{1,0:T(8,128)S(1)}, f32[24,256]{1,0:T(8,128)S(1)}, u32[]{:S(2)}, u32[]{:S(2)}) collective-permute-start(f32[24,256]{1,0:T(8,128)S(1)} %concatenate.6), channel_id=1, source_target_pairs={{2,0},{3,1},{4,2},{5,3},{6,4},{7,5},{0,6},{1,7},{10,8},{11,9},{12,... | collective-permute-start | bytes 73736 | tf_op jit(solution)/shard_map/ppermute | solution.py:18
  22.3 14.3 %collective-permute-start.2 = (f32[24,256]{1,0:T(8,128)S(1)}, f32[24,256]{1,0:T(8,128)S(1)}, u32[]{:S(2)}, u32[]{:S(2)}) collective-permute-start(f32[24,256]{1,0:T(8,128)S(1)} %concatenate.6), channel_id=1, source_target_pairs={{6,0},{7,1},{0,2},{1,3},{2,4},{3,5},{4,6},{5,7},{14,8},{15,9},{8,1... | collective-permute-start | bytes 73736 | tf_op jit(solution)/shard_map/ppermute | solution.py:18
  22.7 14.7 %collective-permute-start.1 = (f32[24,256]{1,0:T(8,128)S(1)}, f32[24,256]{1,0:T(8,128)S(1)}, u32[]{:S(2)}, u32[]{:S(2)}) collective-permute-start(f32[24,256]{1,0:T(8,128)S(1)} %concatenate.6), channel_id=1, source_target_pairs={{1,0},{2,1},{3,2},{4,3},{5,4},{6,5},{7,6},{0,7},{9,8},{10,9},{11,1... | collective-permute-start | bytes 73736 | tf_op jit(solution)/shard_map/ppermute | solution.py:18
  26.5 13.5 %collective-permute-start = (f32[24,256]{1,0:T(8,128)S(1)}, f32[24,256]{1,0:T(8,128)S(1)}, u32[]{:S(2)}, u32[]{:S(2)}) collective-permute-start(f32[24,256]{1,0:T(8,128)S(1)} %concatenate.6), channel_id=1, source_target_pairs={{7,0},{0,1},{1,2},{2,3},{3,4},{4,5},{5,6},{6,7},{15,8},{8,9},{9,10... | collective-permute-start | bytes 73736 | tf_op jit(solution)/shard_map/ppermute | solution.py:18
  30.2 41.1 %all-to-all-start = ((f32[5,4,3240]{2,0,1:T(8,128)}), f32[5,4,3240]{2,0,1:T(8,128)S(1)}, u32[]{:S(2)}, u32[]{:S(2)}) async-start(f32[5,4,3240]{2,0,1:T(8,128)} %copy.29), calls=%async_computation | async-start | bytes 851968 | tf_op jit(solution)/shard_map/all_to_all | solution.py:118
  71.3 0.8 copy-start
where the time goes:
time: 105 us
  matrix products  28.1 us (27%)
  local copies, waits for them, and re-layouts  27.2 us (26%)
  blocking collectives  24.3 us (23%)
  starting transfers between devices  11.7 us (11%)
  other arithmetic  7.44 us (7%)
  between operations  5.13 us (5%)
    all_to_all x1, blocking collectives, shards(): lax.all_to_all(analysis[:, None, :], 'mem', split_axis=0, concat_axis=1,...  13.5 us
    all_gather x1, blocking collectives, shards(): ensemble = lax.all_gather(own_obs, 'mem', axis=0, tiled=True)  10.8 us
    dot_general x6, matrix products, add_block(): jnp.einsum('pkj,lj->pkl', weighted, spread_obs, precision=highest)  8.91 us
    another operation x2, local copies, waits for them, and re-layouts, apply_mix(): band_state.reshape(members, row_blocks, BLOCK, col_blocks, BLOCK)  8.62 us
    ppermute x4, starting transfers between devices, shifted(): return lax.ppermute(block, axis, route)  7.34 us
    unnamed x17, local copies, waits for them, and re-layouts  5.97 us
    dot_general x1, matrix products, apply_mix(): jnp.einsum('ablk,laibj->kaibj', mix_blocks, spread_state, precision=highest)  4.5 us
    all_to_all x1, starting transfers between devices, shards(): lax.all_to_all(spread, 'mem', split_axis=1, concat_axis=0, tiled=True)  4.35 us
  transfers between devices with their start and end apart: 5, of which 0 were waited for; matrix products, arithmetic and copies ran while one was open for 32% of the time, Pallas kernels for 0%

commit v1 on v0

v1 whole, which is shorter than its diff:
```python
import functools
import math

import jax
import jax.numpy as jnp
import numpy as np
from jax import lax
from jax.experimental import pallas as pl
from jax.experimental.pallas import tpu as pltpu
from jax.sharding import PartitionSpec as P

COLS = 45
BLOCK = 9
HALO = 2
NS_ITERS = 4
LANES = 128
MESH = pl.DeviceIdType.MESH


def ceil_to(x, m):
    return (x + m - 1) // m * m


def split(x, parts):
    out = []
    for _ in range(parts):
        piece = x.astype(jnp.bfloat16)
        out.append(piece)
        x = x - piece.astype(jnp.float32)
    return out


def dot(a, b):
    return jnp.dot(a, b, preferred_element_type=jnp.float32)


def dot_nt(a, b):
    return lax.dot_general(a, b, (((1,), (1,)), ((), ())), preferred_element_type=jnp.float32)


def iota(shape, dim):
    return lax.broadcasted_iota(jnp.int32, shape, dim)


def kernel(
    dims,
    count_ref, radius_ref, state_ref, index_ref, value_ref, rinv_ref, block_ref,
    out_ref,
    own_ref, obs_ref, recv_ref, back_ref, pert_ref, prs_ref, gram_ref, y_ref, z_ref, m_ref, t_ref,
    vec_ref, obs_send, obs_recv, st_send, st_recv, bk_send, bk_recv,
):
    groups, tiles, mem_dev, slots, band_cells, width, points = dims
    members = groups * mem_dev
    mpad = gram_ref.shape[1]
    rows_dev = band_cells // COLS
    col_blocks = COLS // BLOCK
    me = lax.axis_index("mem")
    tile = lax.axis_index("tile")
    offsets = list(range(-HALO, HALO + 1))
    peers = [(s, d) for d in offsets for s in range(groups) if (s, d) != (0, 0)]

    def member(s):
        return lax.rem(me + s, groups)

    def column(d):
        return lax.rem(tile + d + tiles, tiles)

    barrier = pltpu.get_barrier_semaphore()
    for s, d in peers:
        pl.semaphore_signal(barrier, inc=1, device_id=(member(s), column(d)), device_id_type=MESH)

    cell = index_ref[...]
    cell_f = cell.astype(jnp.float32)
    band = jnp.floor((cell_f + 0.5) * (1.0 / band_cells))
    inside = cell_f - band * band_cells
    strip = jnp.floor((inside + 0.5) * (1.0 / LANES))
    lane = inside - strip * LANES
    strips = width // LANES
    row_id = (band * strips + strip).astype(jnp.int32)
    lane_id = lane.astype(jnp.int32)
    lane_hot = jnp.where(iota((LANES, slots), 0) == lane_id, 1.0, 0.0).astype(jnp.bfloat16)
    dev_pad = ceil_to(mem_dev, 8)
    pieces = []
    for b in range(groups):
        rows = state_ref[b]
        if dev_pad > mem_dev:
            rows = jnp.concatenate([rows, jnp.zeros((dev_pad - mem_dev, width), jnp.float32)], axis=0)
        for r in range(strips):
            pieces.append(rows[:, r * LANES : (r + 1) * LANES])
    table = jnp.concatenate(pieces, axis=0)
    picked = sum(dot(part, lane_hot) for part in split(table, 3))
    own = jnp.zeros((dev_pad, slots), jnp.float32)
    for r in range(groups * strips):
        own = own + jnp.where(row_id == r, picked[r * dev_pad : (r + 1) * dev_pad], 0.0)
    live = jnp.where(iota((1, slots), 1) < count_ref[0], rinv_ref[...], 0.0)
    payload = jnp.concatenate([own[:mem_dev], value_ref[...], live, cell_f], axis=0)
    own_ref[...] = payload
    obs_ref[me, HALO] = payload
    recv_ref[me] = state_ref[me]

    pl.semaphore_wait(barrier, len(peers))

    def obs_copy(n, s, d):
        return pltpu.make_async_remote_copy(
            src_ref=own_ref,
            dst_ref=obs_ref.at[me, HALO - d],
            send_sem=obs_send.at[n],
            recv_sem=obs_recv.at[me, HALO - d],
            device_id=(member(s), column(d)),
            device_id_type=MESH,
        )

    def obs_wait(n, s, d):
        src = member(s)
        return pltpu.make_async_remote_copy(
            src_ref=own_ref,
            dst_ref=obs_ref.at[src, HALO + d],
            send_sem=obs_send.at[n],
            recv_sem=obs_recv.at[src, HALO + d],
            device_id=(src, column(d)),
            device_id_type=MESH,
        )

    def band_copy(s, src_ref, dst_ref, send, recv):
        to = member(s)
        return pltpu.make_async_remote_copy(
            src_ref=src_ref.at[to], dst_ref=dst_ref.at[me], send_sem=send.at[s],
            recv_sem=recv.at[me], device_id=(to, tile), device_id_type=MESH,
        )

    def band_wait(s, src_ref, dst_ref, send, recv):
        to = member(s)
        return pltpu.make_async_remote_copy(
            src_ref=src_ref.at[to], dst_ref=dst_ref.at[to], send_sem=send.at[s],
            recv_sem=recv.at[to], device_id=(to, tile), device_id_type=MESH,
        )

    for n, (s, d) in enumerate(peers):
        obs_copy(n, s, d).start()
    for s in range(1, groups):
        band_copy(s, state_ref, recv_ref, st_send, st_recv).start()
    for n, (s, d) in enumerate(peers):
        obs_wait(n, s, d).wait_recv()

    point = iota((points, 1), 0).astype(jnp.float32)
    point_row = jnp.floor((point + 0.5) * (1.0 / col_blocks))
    point_col = point - point_row * col_blocks
    half = (BLOCK - 1) // 2
    prow = point_row * BLOCK + (me * rows_dev + half).astype(jnp.float32)
    pcol = point_col * BLOCK + (tile * COLS + half).astype(jnp.float32)
    extent = jnp.full((1, 1), radius_ref[0] * COLS, jnp.int32).astype(jnp.float32)
    circle = float(COLS * tiles)
    weights = []
    for at, d in enumerate(offsets):
        ens = jnp.concatenate([obs_ref[g, at][:mem_dev] for g in range(groups)], axis=0)
        meta = obs_ref[0, at]
        centre = jnp.sum(ens, axis=0, keepdims=True) * (1.0 / members)
        innovation = meta[mem_dev : mem_dev + 1] - centre
        parts = [ens - centre, innovation]
        if mpad > members + 1:
            parts.append(jnp.zeros((mpad - members - 1, slots), jnp.float32))
        pert_ref[:, at * slots : (at + 1) * slots] = jnp.concatenate(parts, axis=0)
        where = meta[mem_dev + 2 : mem_dev + 3]
        obs_row = jnp.floor((where + 0.5) * (1.0 / COLS))
        obs_col = where - obs_row * COLS + (column(d) * COLS).astype(jnp.float32)
        rgap = jnp.abs(obs_row - prow)
        cgap = jnp.abs(obs_col - pcol)
        cgap = jnp.minimum(cgap, circle - cgap)
        taper = jnp.maximum(0.0, 1.0 - rgap / extent) * jnp.maximum(0.0, 1.0 - cgap / extent)
        weights.append(taper * meta[mem_dev + 1 : mem_dev + 2])
    w_hi, w_lo = split(jnp.concatenate(weights, axis=1), 2)

    batch = prs_ref.shape[0] // mpad

    def gram_group(i, _):
        for k in range(batch):
            prs_ref[k * mpad : (k + 1) * mpad] = pert_ref[pl.ds(i * batch + k, 1)] * pert_ref[...]
        p_hi, p_lo = split(prs_ref[...], 2)
        total = dot_nt(p_hi, w_hi) + dot_nt(p_hi, w_lo) + dot_nt(p_lo, w_hi)
        for k in range(batch):
            gram_ref[i * batch + k] = total[k * mpad : (k + 1) * mpad]
        return 0

    if batch == members:
        gram_group(0, 0)
    else:
        lax.fori_loop(0, members // batch, gram_group, 0)

    full = (members, mpad, points)
    eye = jnp.where(iota((members, mpad, 1), 0) == iota((members, mpad, 1), 1), 1.0, 0.0)
    inside_rows = iota((1, mpad, 1), 1) < members
    g = jnp.where(inside_rows, gram_ref[...], 0.0) + (members - 1.0) * eye
    frob = jnp.sqrt(jnp.sum(jnp.sum(g * g, axis=0), axis=0, keepdims=True))
    y_ref[...] = g / frob[None]
    z_ref[...] = 1.5 * eye - 0.5 * y_ref[...]

    step = 4 if members % 4 == 0 else 1

    def product(a_ref, b_ref, o_ref, finish):
        def body(i, _):
            rows = [i * step + u for u in range(step)]
            acc = [None] * step
            for k in range(members):
                right = b_ref[k]
                for u in range(step):
                    term = a_ref[rows[u], k : k + 1, :] * right
                    acc[u] = term if acc[u] is None else acc[u] + term
            for u in range(step):
                o_ref[rows[u]] = finish(rows[u], acc[u])
            return 0

        lax.fori_loop(0, members // step, body, 0)

    def keep(_, x):
        return x

    def middle(i, x):
        return jnp.where(iota((mpad, 1), 0) == i, 1.5, 0.0) - 0.5 * x

    product(y_ref, z_ref, t_ref, keep)
    y, y_other, z, z_other = t_ref, y_ref, z_ref, None
    spare = [y_other]
    for sweep in range(1, NS_ITERS):
        product(z, y, m_ref, middle)
        if sweep < NS_ITERS - 1:
            new_y = spare.pop()
            product(y, m_ref, new_y, keep)
            old_y = y
            product(m_ref, z, old_y, keep)
            spare.append(z)
            y, z = new_y, old_y
        else:
            new_z = spare.pop()
            product(m_ref, z, new_z, keep)
            z = new_z
    root = z[...] * (1.0 / jnp.sqrt(frob))[None]
    z[...] = root
    inner = sum(z[k] * gram_ref[k, members : members + 1, :] for k in range(members))
    vec_ref[...] = inner
    shift = sum(z[k] * vec_ref[k : k + 1, :] for k in range(members))
    vec_ref[...] = shift
    scale = math.sqrt(members - 1.0)
    for l in range(members):
        z[l] = scale * z[l] + vec_ref[l : l + 1, :]

    for s in range(1, groups):
        band_wait(s, state_ref, recv_ref, st_send, st_recv).wait_recv()
    chunk = 2 * LANES if width % (2 * LANES) == 0 else LANES

    def mix_chunk(c, _):
        span = pl.ds(pl.multiple_of(c * chunk, chunk), chunk)
        hot = jnp.where(iota((points, chunk), 0) == block_ref[:, span], 1.0, 0.0).astype(jnp.bfloat16)
        total = jnp.zeros((1, chunk), jnp.float32)
        for g in range(groups):
            total = total + jnp.sum(recv_ref[g, :, span], axis=0, keepdims=True)
        mean = total * (1.0 / members)
        acc = jnp.broadcast_to(mean, (mpad, chunk))
        for l0 in range(0, members, batch):
            mix = z[l0 : l0 + batch].reshape(batch * mpad, points)
            spread = sum(dot(part, hot) for part in split(mix, 2))
            for l in range(batch):
                q, r = divmod(l0 + l, mem_dev)
                dev = recv_ref[q, r : r + 1, span] - mean
                acc = acc + spread[l * mpad : (l + 1) * mpad] * dev
        for g in range(groups):
            back_ref[g, :, span] = acc[g * mem_dev : (g + 1) * mem_dev]
        return 0

    lax.fori_loop(0, width // chunk, mix_chunk, 0)
    for s in range(1, groups):
        band_copy(s, back_ref, out_ref, bk_send, bk_recv).start()
    out_ref[me] = back_ref[me]
    for n, (s, d) in enumerate(peers):
        obs_copy(n, s, d).wait_send()
    for s in range(1, groups):
        band_copy(s, state_ref, recv_ref, st_send, st_recv).wait_send()
    for s in range(1, groups):
        band_wait(s, back_ref, out_ref, bk_send, bk_recv).wait()


def shards(groups, tiles, state, obs_index, obs_count, obs_value, obs_rinv, radius):
    mem_dev, _, cells = state.shape
    slots = obs_index.shape[1]
    members = groups * mem_dev
    band_cells = cells // groups
    width = ceil_to(band_cells, LANES)
    points = (band_cells // COLS // BLOCK) * (COLS // BLOCK)
    mpad = ceil_to(members + 1, 8)
    window = (2 * HALO + 1) * slots
    batch = max(b for b in range(1, members + 1) if members % b == 0 and (b == 1 or b * mpad <= 512))
    bands = state.reshape(mem_dev, groups, band_cells).transpose(1, 0, 2)
    bands = jnp.pad(bands, ((0, 0), (0, 0), (0, width - band_cells)))
    at = np.arange(width)
    block_of = (at // COLS // BLOCK) * (COLS // BLOCK) + at % COLS // BLOCK
    block_of = jnp.asarray(block_of[None].astype(np.int32))
    dims = (groups, tiles, mem_dev, slots, band_cells, width, points)
    peers = groups * (2 * HALO + 1) - 1
    f32 = jnp.float32
    vmem = pl.BlockSpec(memory_space=pltpu.VMEM)
    smem = pl.BlockSpec(memory_space=pltpu.SMEM)
    banded = (groups, mem_dev, width)
    square = pltpu.VMEM((members, mpad, points), f32)
    dma = pltpu.SemaphoreType.DMA
    out = pl.pallas_call(
        functools.partial(kernel, dims),
        out_shape=jax.ShapeDtypeStruct(banded, f32),
        in_specs=[smem, smem] + [vmem] * 5,
        out_specs=vmem,
        scratch_shapes=[
            pltpu.VMEM((mem_dev + 3, slots), f32),
            pltpu.VMEM((groups, 2 * HALO + 1, mem_dev + 3, slots), f32),
            pltpu.VMEM(banded, f32),
            pltpu.VMEM(banded, f32),
            pltpu.VMEM((mpad, window), f32),
            pltpu.VMEM((batch * mpad, window), f32),
            square, square, square, square, square,
            pltpu.VMEM((mpad, points), f32),
            dma((peers,)),
            dma((groups, 2 * HALO + 1)),
            dma((groups,)), dma((groups,)), dma((groups,)), dma((groups,)),
        ],
        compiler_params=pltpu.CompilerParams(collective_id=0, has_side_effects=True),
    )(obs_count, radius, bands, obs_index, obs_value, obs_rinv, block_of)
    out = out[:, :, :band_cells].transpose(1, 0, 2)
    return out.reshape(mem_dev, 1, cells)


def solution(mesh):
    in_specs = (
        P("mem", "tile", None),
        P("tile", None),
        P("tile"),
        P("tile", None),
        P("tile", None),
        P("tile"),
    )
    return jax.shard_map(
        functools.partial(shards, mesh.shape["mem"], mesh.shape["tile"]),
        mesh=mesh, in_specs=in_specs, out_specs=P("mem", "tile", None), check_vma=False,
    )
```

time: 105 us -> 41.6 us (0.40)
  the two profiles are of different devices: /device:TPU:5 before, /device:TPU:28 now
where the time goes in v1:
time: 41.6 us; the launch traced here: 41.4 us
  Pallas kernels  35.1 us (84%)
  local copies, waits for them, and re-layouts  3.4 us (8%)
  other arithmetic  1.58 us (4%)
  between operations  1.33 us (3%)
    pallas_call x1, Pallas kernels, shards(): pl.pallas_call(functools.partial(kernel, dims), out_shape=jax.ShapeDtypeS...  35.1 us
    unnamed x1, other arithmetic  1.58 us
    reshape x1, local copies, waits for them, and re-layouts, shards(): return out.reshape(mem_dev, 1, cells)  1.17 us
    transpose x2, local copies, waits for them, and re-layouts, shards(): out = out[:, :, :band_cells].transpose(1, 0, 2)  1.14 us

profile of v1, /device:TPU:28, one launch (start us, length us, event | category | flops | bytes accessed | tf_op | source)
XLA Modules:
  0.0 41.4 jit_solution(14064602730758238642)
XLA Ops:
  1.3 1.6 %reduce = f32[5,12960]{1,0:T(8,128)S(1)} reduce(f32[5,1,12960]{2,1,0:T(1,128)} %param.7, f32[]{:T(128)} %constant.14), dimensions={1}, to_apply=%param.7.reduce_sub_computation | reduce | bytes 518404 | tf_op args[0]
  2.9 0.2 reshape.6
  3.1 0.1 copy.12
  3.2 0.8 %pad.4.state_ref = f32[4,5,3328]{2,1,0:T(8,128)} pad(f32[4,5,3240]{2,1,0:T(8,128)S(1)} %bitcast.5, f32[]{:T(128)} %constant.4.clone.1), padding=0_0x0_0x0_88 | pad | bytes 525444 | tf_op jit(solution)/shard_map/jit(_pad)/pad | solution.py:292
  4.0 35.1 %shard_map.73 = f32[4,5,3328]{2,1,0:T(8,128)} custom-call(s32[1]{0:T(128)S(6)} %copy.13.count_ref, s32[1]{0:T(128)S(6)} %copy.14.radius_ref, f32[4,5,3328]{2,1,0:T(8,128)} %pad.4.state_ref, s32[1,256]{1,0:T(1,128)} %index_ref.1, f32[1,256]{1,0:T(1,128)} %value_ref.1, f32[1,256]{1,0:T(1,128)} %rinv_ref.1, s32[1,3328]{1,0:T(1,128)} %constant.5.clone.block_ref), custom_call_target="tpu_custom_call" | custom-call | tf_op jit(solution)/shard_map/pallas_call | solution.py:304
  39.1 1.0 %slice_bitcast_fusion = f32[5,4,3240]{2,0,1:T(8,128)S(1)} fusion(f32[4,5,3328]{2,1,0:T(8,128)} %shard_map.73), kind=kLoop, calls=%fused_computation.1 | loop fusion | bytes 518400 | tf_op jit(solution)/shard_map/transpose | solution.py:324
  40.1 0.1 copy.9
  40.3 1.2 %reshape.8 = f32[5,1,12960]{2,1,0:T(1,128)} reshape(f32[5,4,3240]{2,1,0:T(4,128)S(1)} %copy.9) | data formatting | bytes 518400 | tf_op jit(solution)/shard_map/reshape | solution.py:325

commit v2 on v1

--- a/solution.py
+++ b/solution.py
@@ -14,6 +14,7 @@
 HALO = 2
 NS_ITERS = 4
 LANES = 128
+SEGMENTS = 4
 MESH = pl.DeviceIdType.MESH
 
 
@@ -46,8 +47,8 @@
     dims,
     count_ref, radius_ref, state_ref, index_ref, value_ref, rinv_ref, block_ref,
     out_ref,
-    own_ref, obs_ref, recv_ref, back_ref, pert_ref, prs_ref, gram_ref, y_ref, z_ref, m_ref, t_ref,
-    vec_ref, obs_send, obs_recv, st_send, st_recv, bk_send, bk_recv,
+    own_ref, own_meta_ref, obs_ref, meta_ref, recv_ref, back_ref, pert_ref, prs_ref, gram_ref, y_ref, z_ref, m_ref, t_ref,
+    vec_ref, obs_send, obs_recv, meta_send, meta_recv, st_send, st_recv, bk_send, bk_recv,
 ):
     groups, tiles, mem_dev, slots, band_cells, width, points = dims
     members = groups * mem_dev
@@ -93,9 +94,11 @@
     for r in range(groups * strips):
         own = own + jnp.where(row_id == r, picked[r * dev_pad : (r + 1) * dev_pad], 0.0)
     live = jnp.where(iota((1, slots), 1) < count_ref[0], rinv_ref[...], 0.0)
-    payload = jnp.concatenate([own[:mem_dev], value_ref[...], live, cell_f], axis=0)
-    own_ref[...] = payload
-    obs_ref[me, HALO] = payload
+    own_ref[...] = own[:mem_dev]
+    obs_ref[me, HALO] = own[:mem_dev]
+    about = jnp.concatenate([value_ref[...], live, cell_f], axis=0)
+    own_meta_ref[...] = about
+    meta_ref[HALO] = about
     recv_ref[me] = state_ref[me]
 
     pl.semaphore_wait(barrier, len(peers))
@@ -121,24 +124,48 @@
             device_id_type=MESH,
         )
 
-    def band_copy(s, src_ref, dst_ref, send, recv):
+    def meta_copy(d, slot, from_tile):
+        return pltpu.make_async_remote_copy(
+            src_ref=own_meta_ref, dst_ref=meta_ref.at[slot], send_sem=meta_send.at[HALO + d],
+            recv_sem=meta_recv.at[slot], device_id=(me, from_tile), device_id_type=MESH,
+        )
+
+    chunk = 2 * LANES if width % (2 * LANES) == 0 else LANES
+    chunks = width // chunk
+    bounds = [chunks * i // SEGMENTS for i in range(SEGMENTS + 1)]
+    segments = [(a, b) for a, b in zip(bounds, bounds[1:]) if b > a]
+
+    def lanes_of(i):
+        a, b = segments[i]
+        return pl.ds(a * chunk, (b - a) * chunk)
+
+    def band_copy(s, i, src_ref, dst_ref, send, recv):
         to = member(s)
         return pltpu.make_async_remote_copy(
-            src_ref=src_ref.at[to], dst_ref=dst_ref.at[me], send_sem=send.at[s],
-            recv_sem=recv.at[me], device_id=(to, tile), device_id_type=MESH,
-        )
-
-    def band_wait(s, src_ref, dst_ref, send, recv):
+            src_ref=src_ref.at[to, :, lanes_of(i)], dst_ref=dst_ref.at[me, :, lanes_of(i)],
+            send_sem=send.at[s, i], recv_sem=recv.at[me, i],
+            device_id=(to, tile), device_id_type=MESH,
+        )
+
+    def band_wait(s, i, src_ref, dst_ref, send, recv):
         to = member(s)
         return pltpu.make_async_remote_copy(
-            src_ref=src_ref.at[to], dst_ref=dst_ref.at[to], send_sem=send.at[s],
-            recv_sem=recv.at[to], device_id=(to, tile), device_id_type=MESH,
-        )
+            src_ref=src_ref.at[to, :, lanes_of(i)], dst_ref=dst_ref.at[to, :, lanes_of(i)],
+            send_sem=send.at[s, i], recv_sem=recv.at[to, i],
+            device_id=(to, tile), device_id_type=MESH,
+        )
+
+    near = [d for d in offsets if d != 0]
+    for d in near:
+        meta_copy(d, HALO - d, column(d)).start()
 
     for n, (s, d) in enumerate(peers):
         obs_copy(n, s, d).start()
-    for s in range(1, groups):
-        band_copy(s, state_ref, recv_ref, st_send, st_recv).start()
+    for i in range(len(segments)):
+        for s in range(1, groups):
+            band_copy(s, i, state_ref, recv_ref, st_send, st_recv).start()
+    for d in near:
+        meta_copy(d, HALO + d, column(d)).wait_recv()
     for n, (s, d) in enumerate(peers):
         obs_wait(n, s, d).wait_recv()
 
@@ -152,22 +179,22 @@
     circle = float(COLS * tiles)
     weights = []
     for at, d in enumerate(offsets):
-        ens = jnp.concatenate([obs_ref[g, at][:mem_dev] for g in range(groups)], axis=0)
-        meta = obs_ref[0, at]
+        ens = jnp.concatenate([obs_ref[g, at] for g in range(groups)], axis=0)
+        meta = meta_ref[at]
         centre = jnp.sum(ens, axis=0, keepdims=True) * (1.0 / members)
-        innovation = meta[mem_dev : mem_dev + 1] - centre
+        innovation = meta[0:1] - centre
         parts = [ens - centre, innovation]
         if mpad > members + 1:
             parts.append(jnp.zeros((mpad - members - 1, slots), jnp.float32))
         pert_ref[:, at * slots : (at + 1) * slots] = jnp.concatenate(parts, axis=0)
-        where = meta[mem_dev + 2 : mem_dev + 3]
+        where = meta[2:3]
         obs_row = jnp.floor((where + 0.5) * (1.0 / COLS))
         obs_col = where - obs_row * COLS + (column(d) * COLS).astype(jnp.float32)
         rgap = jnp.abs(obs_row - prow)
         cgap = jnp.abs(obs_col - pcol)
         cgap = jnp.minimum(cgap, circle - cgap)
         taper = jnp.maximum(0.0, 1.0 - rgap / extent) * jnp.maximum(0.0, 1.0 - cgap / extent)
-        weights.append(taper * meta[mem_dev + 1 : mem_dev + 2])
+        weights.append(taper * meta[1:2])
     w_hi, w_lo = split(jnp.concatenate(weights, axis=1), 2)
 
     batch = prs_ref.shape[0] // mpad
@@ -243,10 +270,6 @@
     for l in range(members):
         z[l] = scale * z[l] + vec_ref[l : l + 1, :]
 
-    for s in range(1, groups):
-        band_wait(s, state_ref, recv_ref, st_send, st_recv).wait_recv()
-    chunk = 2 * LANES if width % (2 * LANES) == 0 else LANES
-
     def mix_chunk(c, _):
         span = pl.ds(pl.multiple_of(c * chunk, chunk), chunk)
         hot = jnp.where(iota((points, chunk), 0) == block_ref[:, span], 1.0, 0.0).astype(jnp.bfloat16)
@@ -266,16 +289,23 @@
             back_ref[g, :, span] = acc[g * mem_dev : (g + 1) * mem_dev]
         return 0
 
-    lax.fori_loop(0, width // chunk, mix_chunk, 0)
-    for s in range(1, groups):
-        band_copy(s, back_ref, out_ref, bk_send, bk_recv).start()
+    for i, (first, last) in enumerate(segments):
+        for s in range(1, groups):
+            band_wait(s, i, state_ref, recv_ref, st_send, st_recv).wait_recv()
+        lax.fori_loop(first, last, mix_chunk, 0)
+        for s in range(1, groups):
+            band_copy(s, i, back_ref, out_ref, bk_send, bk_recv).start()
     out_ref[me] = back_ref[me]
     for n, (s, d) in enumerate(peers):
         obs_copy(n, s, d).wait_send()
-    for s in range(1, groups):
-        band_copy(s, state_ref, recv_ref, st_send, st_recv).wait_send()
-    for s in range(1, groups):
-        band_wait(s, back_ref, out_ref, bk_send, bk_recv).wait()
+    for d in near:
+        meta_copy(d, HALO - d, column(d)).wait_send()
+    for i in range(len(segments)):
+        for s in range(1, groups):
+            band_copy(s, i, state_ref, recv_ref, st_send, st_recv).wait_send()
+    for i in range(len(segments)):
+        for s in range(1, groups):
+            band_wait(s, i, back_ref, out_ref, bk_send, bk_recv).wait()
 
 
 def shards(groups, tiles, state, obs_index, obs_count, obs_value, obs_rinv, radius):
@@ -307,8 +337,10 @@
         in_specs=[smem, smem] + [vmem] * 5,
         out_specs=vmem,
         scratch_shapes=[
-            pltpu.VMEM((mem_dev + 3, slots), f32),
-            pltpu.VMEM((groups, 2 * HALO + 1, mem_dev + 3, slots), f32),
+            pltpu.VMEM((mem_dev, slots), f32),
+            pltpu.VMEM((3, slots), f32),
+            pltpu.VMEM((groups, 2 * HALO + 1, mem_dev, slots), f32),
+            pltpu.VMEM((2 * HALO + 1, 3, slots), f32),
             pltpu.VMEM(banded, f32),
             pltpu.VMEM(banded, f32),
             pltpu.VMEM((mpad, window), f32),
@@ -317,7 +349,9 @@
             pltpu.VMEM((mpad, points), f32),
             dma((peers,)),
             dma((groups, 2 * HALO + 1)),
-            dma((groups,)), dma((groups,)), dma((groups,)), dma((groups,)),
+            dma((2 * HALO + 1,)), dma((2 * HALO + 1,)),
+            dma((groups, SEGMENTS)), dma((groups, SEGMENTS)),
+            dma((groups, SEGMENTS)), dma((groups, SEGMENTS)),
         ],
         compiler_params=pltpu.CompilerParams(collective_id=0, has_side_effects=True),
     )(obs_count, radius, bands, obs_index, obs_value, obs_rinv, block_of)

time: 41.6 us -> 40 us (0.962)
  the two profiles are of different devices: /device:TPU:28 before, /device:TPU:0 now
where the time goes in v2:
time: 40 us; the launch traced here: 39.8 us
  Pallas kernels  33.4 us (84%)
  local copies, waits for them, and re-layouts  3.4 us (8%)
  other arithmetic  1.58 us (4%)
  between operations  1.33 us (3%)
    pallas_call x1, Pallas kernels, shards(): pl.pallas_call(functools.partial(kernel, dims), out_shape=jax.ShapeDtypeS...  33.4 us
    unnamed x1, other arithmetic  1.58 us
    reshape x1, local copies, waits for them, and re-layouts, shards(): return out.reshape(mem_dev, 1, cells)  1.17 us
    transpose x2, local copies, waits for them, and re-layouts, shards(): out = out[:, :, :band_cells].transpose(1, 0, 2)  1.14 us

profile of v2, /device:TPU:0, one launch (start us, length us, event | category | flops | bytes accessed | tf_op | source)
XLA Modules:
  0.0 39.8 jit_solution(5616503260579958240)
XLA Ops:
  1.3 1.6 %reduce = f32[5,12960]{1,0:T(8,128)S(1)} reduce(f32[5,1,12960]{2,1,0:T(1,128)} %param.7, f32[]{:T(128)} %constant.14), dimensions={1}, to_apply=%param.7.reduce_sub_computation | reduce | bytes 518404 | tf_op args[0]
  2.9 0.2 reshape.6
  3.1 0.1 copy.12
  3.2 0.8 %pad.4.state_ref = f32[4,5,3328]{2,1,0:T(8,128)} pad(f32[4,5,3240]{2,1,0:T(8,128)S(1)} %bitcast.5, f32[]{:T(128)} %constant.4.clone.1), padding=0_0x0_0x0_88 | pad | bytes 525444 | tf_op jit(solution)/shard_map/jit(_pad)/pad | solution.py:322
  4.0 33.4 %shard_map.73 = f32[4,5,3328]{2,1,0:T(8,128)} custom-call(s32[1]{0:T(128)S(6)} %copy.13.count_ref, s32[1]{0:T(128)S(6)} %copy.14.radius_ref, f32[4,5,3328]{2,1,0:T(8,128)} %pad.4.state_ref, s32[1,256]{1,0:T(1,128)} %index_ref.1, f32[1,256]{1,0:T(1,128)} %value_ref.1, f32[1,256]{1,0:T(1,128)} %rinv_ref.1, s32[1,3328]{1,0:T(1,128)} %constant.5.clone.block_ref), custom_call_target="tpu_custom_call" | custom-call | tf_op jit(solution)/shard_map/pallas_call | solution.py:334
  37.4 1.0 %slice_bitcast_fusion = f32[5,4,3240]{2,0,1:T(8,128)S(1)} fusion(f32[4,5,3328]{2,1,0:T(8,128)} %shard_map.73), kind=kLoop, calls=%fused_computation.1 | loop fusion | bytes 518400 | tf_op jit(solution)/shard_map/transpose | solution.py:358
  38.5 0.1 copy.9
  38.6 1.2 %reshape.8 = f32[5,1,12960]{2,1,0:T(1,128)} reshape(f32[5,4,3240]{2,1,0:T(4,128)S(1)} %copy.9) | data formatting | bytes 518400 | tf_op jit(solution)/shard_map/reshape | solution.py:359

commit v3 on v2

--- a/solution.py
+++ b/solution.py
@@ -14,7 +14,6 @@
 HALO = 2
 NS_ITERS = 4
 LANES = 128
-SEGMENTS = 4
 MESH = pl.DeviceIdType.MESH
 
 
@@ -47,7 +46,7 @@
     dims,
     count_ref, radius_ref, state_ref, index_ref, value_ref, rinv_ref, block_ref,
     out_ref,
-    own_ref, own_meta_ref, obs_ref, meta_ref, recv_ref, back_ref, pert_ref, prs_ref, gram_ref, y_ref, z_ref, m_ref, t_ref,
+    own_ref, own_meta_ref, obs_ref, meta_ref, st_ref, recv_ref, back_ref, res_ref, pert_ref, prs_ref, gram_ref, y_ref, z_ref, m_ref, t_ref,
     vec_ref, obs_send, obs_recv, meta_send, meta_recv, st_send, st_recv, bk_send, bk_recv,
 ):
     groups, tiles, mem_dev, slots, band_cells, width, points = dims
@@ -77,29 +76,35 @@
     strip = jnp.floor((inside + 0.5) * (1.0 / LANES))
     lane = inside - strip * LANES
     strips = width // LANES
-    row_id = (band * strips + strip).astype(jnp.int32)
-    lane_id = lane.astype(jnp.int32)
-    lane_hot = jnp.where(iota((LANES, slots), 0) == lane_id, 1.0, 0.0).astype(jnp.bfloat16)
-    dev_pad = ceil_to(mem_dev, 8)
-    pieces = []
+    lane_hot = jnp.where(iota((LANES, slots), 0) == lane.astype(jnp.int32), 1.0, 0.0)
+    lane_hot = lane_hot.astype(jnp.bfloat16)
+    tall = st_ref.shape[1]
+    row_strip = iota((tall, 1), 0) // mem_dev
+    mine = jnp.where(iota((mem_dev, tall), 1) % mem_dev == iota((mem_dev, tall), 0), 1.0, 0.0)
+    mine = mine.astype(jnp.bfloat16)
+    own = jnp.zeros((mem_dev, slots), jnp.float32)
     for b in range(groups):
         rows = state_ref[b]
-        if dev_pad > mem_dev:
-            rows = jnp.concatenate([rows, jnp.zeros((dev_pad - mem_dev, width), jnp.float32)], axis=0)
         for r in range(strips):
-            pieces.append(rows[:, r * LANES : (r + 1) * LANES])
-    table = jnp.concatenate(pieces, axis=0)
-    picked = sum(dot(part, lane_hot) for part in split(table, 3))
-    own = jnp.zeros((dev_pad, slots), jnp.float32)
-    for r in range(groups * strips):
-        own = own + jnp.where(row_id == r, picked[r * dev_pad : (r + 1) * dev_pad], 0.0)
+            st_ref[b, r * mem_dev : (r + 1) * mem_dev] = rows[:, r * LANES : (r + 1) * LANES]
+        if tall > strips * mem_dev:
+            st_ref[b, strips * mem_dev :] = jnp.zeros((tall - strips * mem_dev, LANES), jnp.float32)
+    for b in range(groups):
+        key = jnp.where(band == b, strip, -1.0).astype(jnp.int32)
+        hit = row_strip == key
+        for part in split(st_ref[b], 3):
+            found = jnp.where(hit, dot(part, lane_hot), 0.0)
+            own = own + dot(mine, found.astype(jnp.bfloat16))
     live = jnp.where(iota((1, slots), 1) < count_ref[0], rinv_ref[...], 0.0)
-    own_ref[...] = own[:mem_dev]
-    obs_ref[me, HALO] = own[:mem_dev]
+    own_ref[...] = own
+    obs_ref[me, HALO] = own
     about = jnp.concatenate([value_ref[...], live, cell_f], axis=0)
     own_meta_ref[...] = about
     meta_ref[HALO] = about
-    recv_ref[me] = state_ref[me]
+    recv_ref[me] = st_ref[me]
+    if tall > strips * mem_dev:
+        pad = jnp.zeros((groups, tall - strips * mem_dev, LANES), jnp.float32)
+        back_ref[:, strips * mem_dev :] = pad
 
     pl.semaphore_wait(barrier, len(peers))
 
@@ -130,19 +135,19 @@
             recv_sem=meta_recv.at[slot], device_id=(me, from_tile), device_id_type=MESH,
         )
 
-    chunk = 2 * LANES if width % (2 * LANES) == 0 else LANES
-    chunks = width // chunk
-    bounds = [chunks * i // SEGMENTS for i in range(SEGMENTS + 1)]
-    segments = [(a, b) for a, b in zip(bounds, bounds[1:]) if b > a]
-
-    def lanes_of(i):
+    per = 2 if strips % 2 == 0 else 1
+    chunk = per * LANES
+    segments = [(a, min(a + 8, strips)) for a in range(0, strips, 8)]
+
+    def rows_of(i):
         a, b = segments[i]
-        return pl.ds(a * chunk, (b - a) * chunk)
+        first = a * mem_dev
+        return pl.ds(first, (tall if b == strips else b * mem_dev) - first)
 
     def band_copy(s, i, src_ref, dst_ref, send, recv):
         to = member(s)
         return pltpu.make_async_remote_copy(
-            src_ref=src_ref.at[to, :, lanes_of(i)], dst_ref=dst_ref.at[me, :, lanes_of(i)],
+            src_ref=src_ref.at[to, rows_of(i)], dst_ref=dst_ref.at[me, rows_of(i)],
             send_sem=send.at[s, i], recv_sem=recv.at[me, i],
             device_id=(to, tile), device_id_type=MESH,
         )
@@ -150,7 +155,7 @@
     def band_wait(s, i, src_ref, dst_ref, send, recv):
         to = member(s)
         return pltpu.make_async_remote_copy(
-            src_ref=src_ref.at[to, :, lanes_of(i)], dst_ref=dst_ref.at[to, :, lanes_of(i)],
+            src_ref=src_ref.at[to, rows_of(i)], dst_ref=dst_ref.at[to, rows_of(i)],
             send_sem=send.at[s, i], recv_sem=recv.at[to, i],
             device_id=(to, tile), device_id_type=MESH,
         )
@@ -163,7 +168,7 @@
         obs_copy(n, s, d).start()
     for i in range(len(segments)):
         for s in range(1, groups):
-            band_copy(s, i, state_ref, recv_ref, st_send, st_recv).start()
+            band_copy(s, i, st_ref, recv_ref, st_send, st_recv).start()
     for d in near:
         meta_copy(d, HALO + d, column(d)).wait_recv()
     for n, (s, d) in enumerate(peers):
@@ -273,39 +278,51 @@
     def mix_chunk(c, _):
         span = pl.ds(pl.multiple_of(c * chunk, chunk), chunk)
         hot = jnp.where(iota((points, chunk), 0) == block_ref[:, span], 1.0, 0.0).astype(jnp.bfloat16)
-        total = jnp.zeros((1, chunk), jnp.float32)
-        for g in range(groups):
-            total = total + jnp.sum(recv_ref[g, :, span], axis=0, keepdims=True)
+
+        def cells(l):
+            q, r = divmod(l, mem_dev)
+            rows = [recv_ref[q, pl.ds((c * per + j) * mem_dev + r, 1)] for j in range(per)]
+            return jnp.concatenate(rows, axis=1)
+
+        total = sum(cells(l) for l in range(members))
         mean = total * (1.0 / members)
         acc = jnp.broadcast_to(mean, (mpad, chunk))
         for l0 in range(0, members, batch):
             mix = z[l0 : l0 + batch].reshape(batch * mpad, points)
             spread = sum(dot(part, hot) for part in split(mix, 2))
             for l in range(batch):
-                q, r = divmod(l0 + l, mem_dev)
-                dev = recv_ref[q, r : r + 1, span] - mean
+                dev = cells(l0 + l) - mean
                 acc = acc + spread[l * mpad : (l + 1) * mpad] * dev
         for g in range(groups):
-            back_ref[g, :, span] = acc[g * mem_dev : (g + 1) * mem_dev]
+            part = acc[g * mem_dev : (g + 1) * mem_dev]
+            for j in range(per):
+                back_ref[g, pl.ds((c * per + j) * mem_dev, mem_dev)] = part[:, j * LANES : (j + 1) * LANES]
         return 0
 
     for i, (first, last) in enumerate(segments):
         for s in range(1, groups):
-            band_wait(s, i, state_ref, recv_ref, st_send, st_recv).wait_recv()
-        lax.fori_loop(first, last, mix_chunk, 0)
-        for s in range(1, groups):
-            band_copy(s, i, back_ref, out_ref, bk_send, bk_recv).start()
-    out_ref[me] = back_ref[me]
+            band_wait(s, i, st_ref, recv_ref, st_send, st_recv).wait_recv()
+        lax.fori_loop(first // per, last // per, mix_chunk, 0)
+        for s in range(1, groups):
+            band_copy(s, i, back_ref, res_ref, bk_send, bk_recv).start()
+
+    def deliver(g, src_ref, i):
+        for r in range(*segments[i]):
+            out_ref[g, :, r * LANES : (r + 1) * LANES] = src_ref[g, r * mem_dev : (r + 1) * mem_dev]
+
+    for i in range(len(segments)):
+        deliver(me, back_ref, i)
     for n, (s, d) in enumerate(peers):
         obs_copy(n, s, d).wait_send()
     for d in near:
         meta_copy(d, HALO - d, column(d)).wait_send()
     for i in range(len(segments)):
         for s in range(1, groups):
-            band_copy(s, i, state_ref, recv_ref, st_send, st_recv).wait_send()
+            band_copy(s, i, st_ref, recv_ref, st_send, st_recv).wait_send()
     for i in range(len(segments)):
         for s in range(1, groups):
-            band_wait(s, i, back_ref, out_ref, bk_send, bk_recv).wait()
+            band_wait(s, i, back_ref, res_ref, bk_send, bk_recv).wait()
+            deliver(member(s), res_ref, i)
 
 
 def shards(groups, tiles, state, obs_index, obs_count, obs_value, obs_rinv, radius):
@@ -330,6 +347,9 @@
     smem = pl.BlockSpec(memory_space=pltpu.SMEM)
     banded = (groups, mem_dev, width)
     square = pltpu.VMEM((members, mpad, points), f32)
+    tall = ceil_to(width // LANES * mem_dev, 8)
+    dense = pltpu.VMEM((groups, tall, LANES), f32)
+    parts = -(-(width // LANES) // 8)
     dma = pltpu.SemaphoreType.DMA
     out = pl.pallas_call(
         functools.partial(kernel, dims),
@@ -341,8 +361,7 @@
             pltpu.VMEM((3, slots), f32),
             pltpu.VMEM((groups, 2 * HALO + 1, mem_dev, slots), f32),
             pltpu.VMEM((2 * HALO + 1, 3, slots), f32),
-            pltpu.VMEM(banded, f32),
-            pltpu.VMEM(banded, f32),
+            dense, dense, dense, dense,
             pltpu.VMEM((mpad, window), f32),
             pltpu.VMEM((batch * mpad, window), f32),
             square, square, square, square, square,
@@ -350,8 +369,8 @@
             dma((peers,)),
             dma((groups, 2 * HALO + 1)),
             dma((2 * HALO + 1,)), dma((2 * HALO + 1,)),
-            dma((groups, SEGMENTS)), dma((groups, SEGMENTS)),
-            dma((groups, SEGMENTS)), dma((groups, SEGMENTS)),
+            dma((groups, parts)), dma((groups, parts)),
+            dma((groups, parts)), dma((groups, parts)),
         ],
         compiler_params=pltpu.CompilerParams(collective_id=0, has_side_effects=True),
     )(obs_count, radius, bands, obs_index, obs_value, obs_rinv, block_of)

time: 40 us -> 37.2 us (0.930)
  Pallas kernels: 33.4 us -> 30.7 us
    pallas_call x1, Pallas kernels: 33.4 us -> 30.7 us  [shards(): pl.pallas_call(functools.partial(kernel, dims), out_shape=jax.ShapeDtypeS...]
where the time goes in v3:
time: 37.2 us; the launch traced here: 37 us
  Pallas kernels  30.7 us (83%)
  local copies, waits for them, and re-layouts  3.4 us (9%)
  other arithmetic  1.58 us (4%)
  between operations  1.33 us (4%)
    pallas_call x1, Pallas kernels, shards(): pl.pallas_call(functools.partial(kernel, dims), out_shape=jax.ShapeDtypeS...  30.7 us
    unnamed x1, other arithmetic  1.58 us
    reshape x1, local copies, waits for them, and re-layouts, shards(): return out.reshape(mem_dev, 1, cells)  1.17 us
    transpose x2, local copies, waits for them, and re-layouts, shards(): out = out[:, :, :band_cells].transpose(1, 0, 2)  1.14 us
    pad x1, local copies, waits for them, and re-layouts, shards(): bands = jnp.pad(bands, ((0, 0), (0, 0), (0, width - band_cells)))  0.78 us

profile of v3, /device:TPU:0, one launch (start us, length us, event | category | flops | bytes accessed | tf_op | source)
XLA Modules:
  0.0 37.0 jit_solution(5522487234192961217)
XLA Ops:
  1.3 1.6 %reduce = f32[5,12960]{1,0:T(8,128)S(1)} reduce(f32[5,1,12960]{2,1,0:T(1,128)} %param.7, f32[]{:T(128)} %constant.14), dimensions={1}, to_apply=%param.7.reduce_sub_computation | reduce | bytes 518404 | tf_op args[0]
  2.9 0.2 reshape.6
  3.1 0.1 copy.12
  3.2 0.8 %pad.4.state_ref = f32[4,5,3328]{2,1,0:T(8,128)} pad(f32[4,5,3240]{2,1,0:T(8,128)S(1)} %bitcast.5, f32[]{:T(128)} %constant.4.clone.1), padding=0_0x0_0x0_88 | pad | bytes 525444 | tf_op jit(solution)/shard_map/jit(_pad)/pad | solution.py:339
  4.0 30.7 %shard_map.73 = f32[4,5,3328]{2,1,0:T(8,128)} custom-call(s32[1]{0:T(128)S(6)} %copy.13.count_ref, s32[1]{0:T(128)S(6)} %copy.14.radius_ref, f32[4,5,3328]{2,1,0:T(8,128)} %pad.4.state_ref, s32[1,256]{1,0:T(1,128)} %index_ref.1, f32[1,256]{1,0:T(1,128)} %value_ref.1, f32[1,256]{1,0:T(1,128)} %rinv_ref.1, s32[1,3328]{1,0:T(1,128)} %constant.5.clone.block_ref), custom_call_target="tpu_custom_call" | custom-call | tf_op jit(solution)/shard_map/pallas_call | solution.py:354
  34.7 1.0 %slice_bitcast_fusion = f32[5,4,3240]{2,0,1:T(8,128)S(1)} fusion(f32[4,5,3328]{2,1,0:T(8,128)} %shard_map.73), kind=kLoop, calls=%fused_computation.1 | loop fusion | bytes 518400 | tf_op jit(solution)/shard_map/transpose | solution.py:377
  35.7 0.1 copy.9
  35.8 1.2 %reshape.8 = f32[5,1,12960]{2,1,0:T(1,128)} reshape(f32[5,4,3240]{2,1,0:T(4,128)S(1)} %copy.9) | data formatting | bytes 518400 | tf_op jit(solution)/shard_map/reshape | solution.py:378

commit v4 on v3

--- a/solution.py
+++ b/solution.py
@@ -84,9 +84,13 @@
     mine = mine.astype(jnp.bfloat16)
     own = jnp.zeros((mem_dev, slots), jnp.float32)
     for b in range(groups):
-        rows = state_ref[b]
         for r in range(strips):
-            st_ref[b, r * mem_dev : (r + 1) * mem_dev] = rows[:, r * LANES : (r + 1) * LANES]
+            first = b * band_cells + r * LANES
+            many = min(LANES, band_cells - r * LANES)
+            rows = state_ref[:, 0, first : first + many]
+            if many < LANES:
+                rows = jnp.concatenate([rows, jnp.zeros((mem_dev, LANES - many), jnp.float32)], axis=1)
+            st_ref[b, r * mem_dev : (r + 1) * mem_dev] = rows
         if tall > strips * mem_dev:
             st_ref[b, strips * mem_dev :] = jnp.zeros((tall - strips * mem_dev, LANES), jnp.float32)
     for b in range(groups):
@@ -306,12 +310,7 @@
         for s in range(1, groups):
             band_copy(s, i, back_ref, res_ref, bk_send, bk_recv).start()
 
-    def deliver(g, src_ref, i):
-        for r in range(*segments[i]):
-            out_ref[g, :, r * LANES : (r + 1) * LANES] = src_ref[g, r * mem_dev : (r + 1) * mem_dev]
-
-    for i in range(len(segments)):
-        deliver(me, back_ref, i)
+    res_ref[me] = back_ref[me]
     for n, (s, d) in enumerate(peers):
         obs_copy(n, s, d).wait_send()
     for d in near:
@@ -322,7 +321,11 @@
     for i in range(len(segments)):
         for s in range(1, groups):
             band_wait(s, i, back_ref, res_ref, bk_send, bk_recv).wait()
-            deliver(member(s), res_ref, i)
+    for b in range(groups):
+        for r in range(strips):
+            first = b * band_cells + r * LANES
+            many = min(LANES, band_cells - r * LANES)
+            out_ref[:, 0, first : first + many] = res_ref[b, r * mem_dev : (r + 1) * mem_dev, :many]
 
 
 def shards(groups, tiles, state, obs_index, obs_count, obs_value, obs_rinv, radius):
@@ -335,8 +338,6 @@
     mpad = ceil_to(members + 1, 8)
     window = (2 * HALO + 1) * slots
     batch = max(b for b in range(1, members + 1) if members % b == 0 and (b == 1 or b * mpad <= 512))
-    bands = state.reshape(mem_dev, groups, band_cells).transpose(1, 0, 2)
-    bands = jnp.pad(bands, ((0, 0), (0, 0), (0, width - band_cells)))
     at = np.arange(width)
     block_of = (at // COLS // BLOCK) * (COLS // BLOCK) + at % COLS // BLOCK
     block_of = jnp.asarray(block_of[None].astype(np.int32))
@@ -345,7 +346,6 @@
     f32 = jnp.float32
     vmem = pl.BlockSpec(memory_space=pltpu.VMEM)
     smem = pl.BlockSpec(memory_space=pltpu.SMEM)
-    banded = (groups, mem_dev, width)
     square = pltpu.VMEM((members, mpad, points), f32)
     tall = ceil_to(width // LANES * mem_dev, 8)
     dense = pltpu.VMEM((groups, tall, LANES), f32)
@@ -353,7 +353,7 @@
     dma = pltpu.SemaphoreType.DMA
     out = pl.pallas_call(
         functools.partial(kernel, dims),
-        out_shape=jax.ShapeDtypeStruct(banded, f32),
+        out_shape=jax.ShapeDtypeStruct(state.shape, f32),
         in_specs=[smem, smem] + [vmem] * 5,
         out_specs=vmem,
         scratch_shapes=[
@@ -373,8 +373,7 @@
             dma((groups, parts)), dma((groups, parts)),
         ],
         compiler_params=pltpu.CompilerParams(collective_id=0, has_side_effects=True),
-    )(obs_count, radius, bands, obs_index, obs_value, obs_rinv, block_of)
-    out = out[:, :, :band_cells].transpose(1, 0, 2)
+    )(obs_count, radius, state, obs_index, obs_value, obs_rinv, block_of)
     return out.reshape(mem_dev, 1, cells)
 
 

time: 37.2 us -> 34.3 us (0.922)
  local copies, waits for them, and re-layouts: 3.4 us -> 1.67 us
  other arithmetic: 1.58 us -> 0 us
  Pallas kernels: 30.7 us -> 31.1 us
    unnamed x0 -> x1, local copies, waits for them, and re-layouts: none -> 1.67 us
    unnamed x1 -> x0, other arithmetic: 1.58 us -> none
    reshape x3 -> x0, local copies, waits for them, and re-layouts: 1.48 us -> none  [the longest x1 1.17 us: shards(): return out.reshape(mem_dev, 1, cells)]
    transpose x2 -> x0, local copies, waits for them, and re-layouts: 1.14 us -> none  [shards(): out = out[:, :, :band_cells].transpose(1, 0, 2)]
    pad x1 -> x0, local copies, waits for them, and re-layouts: 0.78 us -> none  [shards(): bands = jnp.pad(bands, ((0, 0), (0, 0), (0, width - band_cells)))]
    pallas_call x1, Pallas kernels: 30.7 us -> 31.1 us  [shards(): pl.pallas_call(functools.partial(kernel, dims), out_shape=jax.ShapeDtypeS...]
where the time goes in v4:
time: 34.3 us; the launch traced here: 34.1 us
  Pallas kernels  31.1 us (91%)
  local copies, waits for them, and re-layouts  1.67 us (5%)
  between operations  1.3 us (4%)
    pallas_call x1, Pallas kernels, shards(): pl.pallas_call(functools.partial(kernel, dims), out_shape=jax.ShapeDtypeS...  31.1 us
    unnamed x1, local copies, waits for them, and re-layouts  1.67 us

profile of v4, /device:TPU:0, one launch (start us, length us, event | category | flops | bytes accessed | tf_op | source)
XLA Modules:
  0.0 34.1 jit_solution(15214896075859620042)
XLA Ops:
  1.3 31.1 %shard_map.73 = f32[5,1,12960]{2,1,0:T(1,128)} custom-call(s32[1]{0:T(128)S(6)} %copy.9.count_ref, s32[1]{0:T(128)S(6)} %copy.10.radius_ref, f32[5,1,12960]{2,1,0:T(1,128)} %state_ref.1, s32[1,256]{1,0:T(1,128)} %index_ref.1, f32[1,256]{1,0:T(1,128)} %value_ref.1, f32[1,256]{1,0:T(1,128)} %rinv_ref.1, s32[1,3328]{1,0:T(1,128)} %constant.2.clone.block_ref), custom_call_target="tpu_custom_call" | custom-call | tf_op jit(solution)/shard_map/pallas_call | solution.py:354
  32.4 1.7 %copy.11 = f32[5,1,12960]{2,1,0:T(1,128)} copy(f32[5,1,12960]{2,1,0:T(1,128)} %shard_map.73) | data formatting | bytes 518400
